TPU v7x, 32 devices: a whole 2x2x4 slice. The times are simulated.
32 devices in a mesh: rows: 8 (over z, y), scen: 4 (over x, core).
Axes of the slice: x: 2, y: 2, z: 4, core: 2. Of those that a mesh axis runs over, the one named last changes fastest.
Arguments:
- inverse: bfloat16 [4096, 16384], P('scen', 'rows'), as said below
- voltage_prev: float32 [64, 16384], P('scen', 'rows'), may hold values from -6 to 6
- line_delay: int32 [8, 16], P('rows'), may hold values from 0 to 4, as said below
- line_bus: int32 [8, 16], P('rows'), may hold values from 0 to 2047
- line_impedance: float32 [8, 16], P('rows'), may hold values from 0.5 to 2, as said below
- line_past: float32 [4, 2, 64, 8, 16], P(None, None, 'scen', 'rows'), may hold values from -6 to 6
- model_dest: int32 [1024, 1], P('rows'), may hold values from 0 to 7; in each aligned block of 128 rows (0 to 127, 128 to 255, ...) at most 32 rows name the same one
- model_bus: int32 [1024], P('rows'), may hold values from 0 to 2047
- model_gain: float32 [1024], P('rows'), may hold values from 0.3 to 3
- model_lag: float32 [1024], P('rows'), may hold values from 0.1 to 0.9
- model_state: float32 [64, 1024], P('scen', 'rows'), may hold values from -6 to 6
- model_source: float32 [6, 64, 1024], P(None, 'scen', 'rows'), may hold values from -6 to 6
- switch_bus: int32 [2, 64, 4], P(None, 'scen'), may hold values from 0 to 4095, as said below
- switch_admittance: float32 [64, 4], P('scen'), may hold values from 0.5 to 4
Outputs:
- voltage: float32 [64, 16384], P('scen', 'rows')
- model_current: float32 [64, 1024], P('scen', 'rows')
Inputs may be any that keep to these rules, and one draw needn't show every extreme that they name: `line_delay`: A line joins end (p, q * 2 + c) with end (q, p * 2 + c), with the same delay and impedance at both ends; no line joins the two devices of one subnetwork; delays of lines run from 2 to 4. `line_impedance`: equal at both ends of a line. `switch_bus`: the two buses of a switched branch differ. `inverse`: each block of 4096 columns is symmetric. `model_dest`: among the models of one index of rows at most 32 name the same index.
All inputs are finite; a program needn't handle non-finite values.
Results may differ from a plain program's by a relative error of at most 0.0024.
The roundings to bfloat16 on the way count: a program that leaves them out, or rounds other values in their place, can miss the bound.
Values may be sent and summed in bfloat16 or wider, within the bound.
A program may use at most 128 MiB of HBM per device.

v0:
```python
import jax
import jax.numpy as jnp
from jax import lax
from jax.sharding import PartitionSpec as P


def swapped(value, axis, apart):
    mask = 2**apart
    pairs = [(source, source ^ mask) for source in range(lax.axis_size(axis))]
    return lax.ppermute(value, axis, pairs)


def slot_table(targets, sections, slots):
    onehot = (targets[:, None] == jnp.arange(sections, dtype=jnp.int32)[None, :]).astype(jnp.int32)
    count = targets.shape[0]
    earlier = (
        jnp.arange(count, dtype=jnp.int32)[None, :] < jnp.arange(count, dtype=jnp.int32)[:, None]
    )
    same = targets[:, None] == targets[None, :]
    rank = jnp.sum((earlier & same).astype(jnp.int32), axis=1)
    return targets * slots + rank


def exact_dot(left, right):
    return jnp.dot(left, right, precision=lax.Precision.HIGHEST)


def per_device(
    inverse,
    voltage_prev,
    line_delay,
    line_bus,
    line_impedance,
    line_past,
    model_dest,
    model_bus,
    model_gain,
    model_lag,
    model_state,
    model_source,
    switch_bus,
    switch_admittance,
):
    n = lax.axis_size("rows")
    groups = lax.axis_size("scen")
    place = lax.axis_index("rows")
    share = lax.axis_index("scen")
    subnet = place // 2
    half = place % 2
    lower = half == 0
    depth_rows, width = inverse.shape
    scen = voltage_prev.shape[0]
    steps = model_source.shape[0]
    ends = line_bus.shape[1]
    models = model_bus.shape[0]
    depth_max = line_past.shape[0]
    slots = max(2, 2 * models // n)
    cap = n * slots
    f32, bf16 = (jnp.float32, jnp.bfloat16)

    def by_half(own, other):
        return jnp.where(
            lower, jnp.concatenate([own, other], -1), jnp.concatenate([other, own], -1)
        )

    slot = slot_table(model_dest[:, 0], n, slots)
    placing = (slot[:, None] == jnp.arange(cap, dtype=jnp.int32)[None, :]).astype(f32)
    bus_out = exact_dot((model_bus + 1).astype(f32)[None], placing)
    bus_out = jnp.broadcast_to(
        bus_out.reshape(n // 2, 1, 2 * slots), (n // 2, 2, 2 * slots)
    ).reshape(n, 2 * slots)
    ends_out = jnp.broadcast_to(line_bus.astype(f32) + 1.0, (n, ends))
    buses = lax.all_to_all(jnp.concatenate([bus_out, ends_out], 1), "rows", 0, 0, tiled=True)
    model_pts = buses[:, : 2 * slots].reshape(n, 2, slots).transpose(1, 0, 2).reshape(2, cap)
    ends_pts = lax.dynamic_slice_in_dim(buses[:, 2 * slots :], subnet * 2, 2, axis=0)
    half_pts = jnp.concatenate([model_pts, ends_pts], 1).astype(jnp.int32) - 1
    pts = jnp.where(half_pts < 0, -1, half_pts + jnp.array([[0], [width]], jnp.int32)).reshape(-1)
    own_pts = lax.dynamic_index_in_dim(half_pts, half, 0, keepdims=False)
    hp = cap + ends
    payload = jnp.concatenate(
        [
            model_lag[None],
            ((1.0 - model_lag) * model_gain)[None],
            model_state,
            model_source.reshape(steps * scen, models),
        ],
        0,
    )
    sent = exact_dot(payload, placing).reshape(-1, n // 2, 1, 2 * slots)
    sent = (
        jnp.broadcast_to(sent, (payload.shape[0], n // 2, 2, 2 * slots))
        .reshape(-1, n, 2 * slots)
        .transpose(1, 0, 2)
    )
    got = lax.all_to_all(sent, "rows", 0, 0, tiled=True)
    got = got.reshape(n, -1, 2, slots).transpose(1, 2, 0, 3).reshape(-1, 2, cap)
    zeros_ends = jnp.zeros((got.shape[0], 2, ends), f32)
    got = jnp.concatenate([got, zeros_ends], 2).reshape(-1, 2 * hp)
    lag, gain, current = (got[0], got[1], got[2 : 2 + scen])
    source = got[2 + scen :].reshape(steps, scen, 2 * hp)
    col_sel = (jnp.arange(width, dtype=jnp.int32)[:, None] == own_pts[None, :]).astype(bf16)
    first_all = lax.dynamic_index_in_dim(
        lax.all_gather(switch_bus[0], "scen", axis=0, tiled=True), subnet, 1, keepdims=False
    )
    second_all = lax.dynamic_index_in_dim(
        lax.all_gather(switch_bus[1], "scen", axis=0, tiled=True), subnet, 1, keepdims=False
    )
    row_ids = jnp.arange(depth_rows, dtype=jnp.int32)[None, :] + share * depth_rows
    col_ids = jnp.arange(width, dtype=jnp.int32)[None, :] + half * width
    picks = (row_ids == first_all[:, None]).astype(bf16) - (row_ids == second_all[:, None]).astype(
        bf16
    )
    col_picks = (col_ids == first_all[:, None]).astype(f32) - (
        col_ids == second_all[:, None]
    ).astype(f32)
    row_sel = (row_ids == pts[:, None]).astype(bf16)
    narrow = jnp.dot(inverse, col_sel, preferred_element_type=f32).astype(bf16)
    part = jnp.dot(row_sel, narrow, preferred_element_type=f32).astype(bf16)
    own_cols = lax.psum(part, "scen")
    branch_part = jnp.dot(picks, inverse, preferred_element_type=f32)
    pts_part = jnp.dot(picks, narrow, preferred_element_type=f32)
    depth_part = jnp.sum(branch_part * col_picks, axis=1, keepdims=True)
    side = lax.psum(jnp.concatenate([pts_part, depth_part], 1), "scen")
    side = lax.dynamic_slice_in_dim(side, share * scen, scen, axis=0)
    own_diag = lax.dynamic_slice_in_dim(own_cols, half * hp, hp, axis=0)
    cross = lax.dynamic_slice_in_dim(own_cols, (1 - half) * hp, hp, axis=0).T
    other_diag = swapped(own_diag, "rows", 0)
    other_cols = jnp.where(
        lower, jnp.concatenate([cross, other_diag], 0), jnp.concatenate([other_diag, cross], 0)
    )
    matrix = by_half(own_cols, other_cols)
    volt0 = exact_dot(voltage_prev, col_sel.astype(f32))
    past = line_past[:, :, :, 0, :].reshape(depth_max * 2 * scen, ends)
    line_info = jnp.concatenate([past, line_delay.astype(f32), line_impedance], 0)
    other_side = swapped(side, "rows", 0)
    other_volt = swapped(volt0, "rows", 0)
    other_info = swapped(line_info, "rows", 0)
    depth = (side + other_side)[:, hp]
    branch = by_half(side[:, :hp], other_side[:, :hp])
    volt = by_half(volt0, other_volt)
    info = jnp.stack([line_info, other_info])
    info = jnp.where(lower, info, info[::-1])
    past = info[:, : depth_max * 2 * scen].reshape(2, depth_max, 2, scen, ends)
    history = [past[:, k] for k in range(depth_max)]
    delays = info[:, -2][:, None, :]
    impedance = info[:, -1][:, None, :]
    admit = lax.dynamic_index_in_dim(switch_admittance, subnet, axis=1, keepdims=False)
    same = pts[:, None] == pts[None, :]
    before = (
        jnp.arange(2 * hp, dtype=jnp.int32)[:, None] < jnp.arange(2 * hp, dtype=jnp.int32)[None, :]
    )
    leading = jnp.sum((same & before).astype(jnp.int32), axis=0) == 0
    merge = (same & leading[None, :]).astype(f32)
    for step in range(steps):
        current = lag * current + gain * (source[step] - volt)
        line_term = jnp.zeros((2, scen, ends), f32)
        for delay in range(2, depth_max + 1):
            older = history[step - delay + depth_max]
            line_term = line_term + jnp.where(
                delays == delay, -(2.0 / impedance) * older[:, 0] - older[:, 1], 0.0
            )
        zeros = jnp.zeros((scen, cap), f32)
        lines = jnp.concatenate([zeros, line_term[0], zeros, line_term[1]], 1)
        rhs = exact_dot(current - lines, merge).astype(bf16)
        along = jnp.sum(rhs.astype(f32) * branch, axis=1)
        factor = admit * along / (1.0 + admit * depth)
        if step + 1 < steps:
            base = jnp.dot(rhs, matrix, preferred_element_type=f32)
            volt = base - factor[:, None] * branch
        if step + 2 < steps:
            own_volt = jnp.where(lower, volt[:, cap:hp], volt[:, hp + cap :])
            own_term = jnp.where(lower, line_term[0], line_term[1])
            out = jnp.stack([own_volt, own_term]).reshape(2, scen, n // 2, 2 * ends // n)
            out = jnp.broadcast_to(
                out.transpose(2, 0, 1, 3)[:, None], (n // 2, 2, 2, scen, 2 * ends // n)
            )
            back = lax.all_to_all(out.reshape(n, 2, scen, 2 * ends // n), "rows", 0, 0, tiled=True)
            back = back.reshape(n, 2, scen, 2, ends // n).transpose(3, 1, 2, 0, 4)
            history.append(back.reshape(2, 2, scen, ends))
    rhs_all = lax.all_gather(rhs, "scen", axis=0, tiled=True)
    factor_all = lax.all_gather(factor[:, None], "scen", axis=0, tiled=True)
    dense = jnp.dot(rhs_all, row_sel, preferred_element_type=f32).astype(bf16)
    partial = jnp.dot(dense, inverse, preferred_element_type=f32) - factor_all * branch_part
    voltage = lax.psum_scatter(partial, "scen", scatter_dimension=0, tiled=True)
    own_current = jnp.where(lower, current[:, :cap], current[:, hp : hp + cap])
    back = lax.all_to_all(
        own_current.reshape(scen, n, slots).transpose(1, 0, 2), "rows", 0, 0, tiled=True
    )
    model_current = lax.dot_general(
        back.transpose(1, 0, 2).reshape(scen, cap),
        placing,
        (((1,), (1,)), ((), ())),
        precision=lax.Precision.HIGHEST,
    )
    return (voltage, model_current)


def solution(mesh):
    placed = (
        P("scen", "rows"),
        P("scen", "rows"),
        P("rows", None),
        P("rows", None),
        P("rows", None),
        P(None, None, "scen", "rows", None),
        P("rows", None),
        P("rows"),
        P("rows"),
        P("rows"),
        P("scen", "rows"),
        P(None, "scen", "rows"),
        P(None, "scen", None),
        P("scen", None),
    )
    return jax.shard_map(
        per_device,
        mesh=mesh,
        in_specs=placed,
        out_specs=(P("scen", "rows"), P("scen", "rows")),
        check_vma=False,
    )
```

profile of v0, /device:TPU:0, one launch (start us, length us, event | category | flops | bytes accessed | tf_op | source)
XLA Modules:
  0.0 226.6 jit_solution(2382398934178793982)
XLA Ops:
  7.2 0.9 convert_reduce_fusion.1
  9.5 1.0 fusion.71
  11.1 7.3 %all-to-all-start.1 = ((f32[8,1,80]{2,1,0:T(1,128)}), f32[8,1,80]{2,1,0:T(1,128)S(1)}, u32[]{:S(2)}, u32[]{:S(2)}) async-start(f32[8,1,80]{2,1,0:T(1,128)} %bitcast.19), calls=%async_computation.1 | async-start | bytes 8192 | tf_op jit(solution)/shard_map/all_to_all | solution.py:73
  18.4 0.7 copy.254
  19.9 0.9 copy.309
  20.8 2.0 collective-permute-start.1
  23.7 5.2 %all-gather.1 = s32[1,64,4]{2,0,1:T(1,128)S(1)} all-gather(s32[1,16,4]{2,0,1:T(1,128)S(1)} %copy.320), channel_id=3, replica_groups=mesh['rows'=8,'scen'=4] {'scen'}, dimensions={1}, use_global_device_ids=true | all-gather | bytes 1280 | tf_op jit(solution)/shard_map/all_gather | solution.py:106
  29.0 5.2 %all-gather = s32[1,64,4]{2,0,1:T(1,128)S(1)} all-gather(s32[1,16,4]{2,0,1:T(1,128)S(1)} %copy.319), channel_id=2, replica_groups=mesh['rows'=8,'scen'=4] {'scen'}, dimensions={1}, use_global_device_ids=true | all-gather | bytes 1280 | tf_op jit(solution)/shard_map/all_gather | solution.py:103
  34.2 1.3 dynamic-slice_reduce_fusion
  35.5 1.3 dynamic-slice_reduce_fusion.1
  37.5 1.2 fusion.66
  38.7 3.2 %multiply_reduce_fusion = (f32[64]{0:T(128)S(1)}, f32[64,2048]{1,0:T(8,128)S(1)}) fusion(s32[2048]{0:T(1024)S(1)} %iota_add_fusion, s32[64]{0:T(128)S(1)} %dynamic-slice_reduce_fusion, s32[64]{0:T(128)S(1)} %dynamic-slice_reduce_fusion.1, bf16[1024,2048]{1,0:T(8,128)(2,1)} %param.15, s32[1024]{0:T(1024)S(1)} %iota_add_fusion.1), kind=kOutput, calls=%fused_computation.54 | convolution fusion | flops 269680576 | bytes 4731648 | tf_op jit(solution)/shard_map/dot_general | solution.py:120
  44.8 4.5 %all-to-all-start = ((f32[8,114,64]{1,2,0:T(8,128)}), f32[8,114,64]{1,2,0:T(8,128)S(1)}, u32[]{:S(2)}, u32[]{:S(2)}) async-start(f32[8,114,64]{1,2,0:T(8,128)} %bitcast.8), calls=%async_computation | async-start | bytes 524288 | tf_op jit(solution)/shard_map/all_to_all | solution.py:95
  49.7 4.1 %fusion.16 = bf16[272,1024]{1,0:T(8,128)(2,1)S(1)} fusion(bf16[1024,2048]{1,0:T(8,128)(2,1)} %param.15, s32[272]{0:T(512)S(1)} %fusion.142), kind=kOutput, calls=%fused_computation.21 | convolution fusion | flops 1142243328 | bytes 4752448 | tf_op jit(solution)/shard_map/dot_general | solution.py:117
  54.4 1.5 fusion.19
  55.9 1.0 fusion.39
  57.7 2.0 collective-permute-start
  62.9 27.9 %all-reduce.5.cloned.1.call-done = bf16[544,272]{0,1:T(8,128)(2,1)} async-done(((bf16[544,272]{0,1:T(8,128)(2,1)}), bf16[544,272]{0,1:T(8,128)(2,1)}) %all-reduce.5.cloned.1.call-update) | async-done | bytes 295952 | tf_op jit(solution)/shard_map/psum | solution.py:119
  90.7 1.3 constant_dynamic-slice_fusion.4
  92.0 1.5 collective-permute-start.2
  93.6 31.6 %all-reduce.7.cloned.1.call-done = f32[64,273]{1,0:T(8,128)} async-done(((f32[64,273]{1,0:T(8,128)}), f32[64,273]{1,0:T(8,128)}) %all-reduce.7.cloned.1.call-update) | async-done | bytes 69904 | tf_op jit(solution)/shard_map/psum | solution.py:123
  125.1 0.7 constant_dynamic-slice_fusion
  125.9 1.5 collective-permute-start.3
  127.4 0.7 constant_dynamic-slice_fusion.1
  128.8 1.2 pad_slice_fusion.1
  130.1 1.1 copy.307
  131.9 1.6 multiply_reduce_fusion.6
  133.8 0.9 fusion.135
  135.2 0.8 multiply_reduce_fusion.5
  137.3 4.6 %all-to-all-start.3 = ((f32[8,1,128]{2,1,0:T(1,128)}), f32[8,1,128]{2,1,0:T(1,128)S(1)}, u32[]{:S(2)}, u32[]{:S(2)}) async-start(f32[8,1,128]{2,1,0:T(1,128)} %reshape.252), calls=%async_computation.3 | async-start | bytes 8192 | tf_op jit(solution)/shard_map/all_to_all | solution.py:177
  143.1 5.2 %all-to-all-done.3 = f32[8,1,128]{2,1,0:T(1,128)S(1)} async-done(((f32[8,1,128]{2,1,0:T(1,128)}), f32[8,1,128]{2,1,0:T(1,128)S(1)}, u32[]{:S(2)}, u32[]{:S(2)}) %all-to-all-start.3) | async-done | bytes 4128 | tf_op jit(solution)/shard_map/all_to_all | solution.py:177
  148.3 3.3 %all-to-all-start.2 = ((f32[8,1,128]{2,1,0:T(1,128)}), f32[8,1,128]{2,1,0:T(1,128)S(1)}, u32[]{:S(2)}, u32[]{:S(2)}) async-start(f32[8,1,128]{2,1,0:T(1,128)} %reshape.250), calls=%async_computation.2 | async-start | bytes 8192 | tf_op jit(solution)/shard_map/all_to_all | solution.py:177
  153.2 4.7 %all-to-all-done.2 = f32[8,1,128]{2,1,0:T(1,128)S(1)} async-done(((f32[8,1,128]{2,1,0:T(1,128)}), f32[8,1,128]{2,1,0:T(1,128)S(1)}, u32[]{:S(2)}, u32[]{:S(2)}) %all-to-all-start.2) | async-done | bytes 4128 | tf_op jit(solution)/shard_map/all_to_all | solution.py:177
  159.1 0.8 multiply_reduce_fusion.4
  160.4 0.8 multiply_reduce_fusion.3
  162.5 3.3 %all-to-all-start.5 = ((f32[8,1,128]{2,1,0:T(1,128)}), f32[8,1,128]{2,1,0:T(1,128)S(1)}, u32[]{:S(2)}, u32[]{:S(2)}) async-start(f32[8,1,128]{2,1,0:T(1,128)} %reshape.256), calls=%async_computation.5 | async-start | bytes 8192 | tf_op jit(solution)/shard_map/all_to_all | solution.py:177
  166.7 5.5 %all-to-all-done.5 = f32[8,1,128]{2,1,0:T(1,128)S(1)} async-done(((f32[8,1,128]{2,1,0:T(1,128)}), f32[8,1,128]{2,1,0:T(1,128)S(1)}, u32[]{:S(2)}, u32[]{:S(2)}) %all-to-all-start.5) | async-done | bytes 4128 | tf_op jit(solution)/shard_map/all_to_all | solution.py:177
  172.2 3.3 %all-to-all-start.4 = ((f32[8,1,128]{2,1,0:T(1,128)}), f32[8,1,128]{2,1,0:T(1,128)S(1)}, u32[]{:S(2)}, u32[]{:S(2)}) async-start(f32[8,1,128]{2,1,0:T(1,128)} %reshape.254), calls=%async_computation.4 | async-start | bytes 8192 | tf_op jit(solution)/shard_map/all_to_all | solution.py:177
  176.5 5.3 %all-to-all-done.4 = f32[8,1,128]{2,1,0:T(1,128)S(1)} async-done(((f32[8,1,128]{2,1,0:T(1,128)}), f32[8,1,128]{2,1,0:T(1,128)S(1)}, u32[]{:S(2)}, u32[]{:S(2)}) %all-to-all-start.4) | async-done | bytes 4128 | tf_op jit(solution)/shard_map/all_to_all | solution.py:177
  182.8 0.8 multiply_reduce_fusion.2
  184.1 0.8 multiply_reduce_fusion.1
  184.9 5.3 %all_gather.14 = bf16[64,544]{1,0:T(8,128)(2,1)S(1)} all-gather(bf16[16,544]{1,0:T(8,128)(2,1)S(1)} %get-tuple-element.76), channel_id=1, replica_groups=mesh['rows'=8,'scen'=4] {'scen'}, dimensions={0}, use_global_device_ids=true | all-gather | bytes 87040 | tf_op jit(solution)/shard_map/all_gather | solution.py:180
  190.6 6.1 %all-reduce.1 = f32[64]{0:T(128)S(1)} all-reduce(f32[64]{0:T(128)S(1)} %dynamic-update-slice), channel_id=1, replica_groups=mesh['rows'=8,'scen'=4] {'scen'}, use_global_device_ids=true, to_apply=%add.1 | all-reduce | flops 64 | bytes 512
  196.7 4.3 %convolution_subtract_fusion = f32[64,2048]{1,0:T(8,128)} fusion(bf16[1024,2048]{1,0:T(8,128)(2,1)} %param.15, bf16[64,544]{1,0:T(8,128)(2,1)S(1)} %all_gather.14, s32[1024]{0:T(1024)S(1)} %iota_add_fusion.1, s32[544]{0:T(1024)S(1)} %select_n.202, f32[64,2048]{1,0:T(8,128)S(1)} %get-tuple-element.65, f32[64]{0:T(128)S(1)} %all-reduce.1), kind=kOutput, calls=%fused_computation.7 | convolution fusion | flops 340623360 | bytes 5319040 | tf_op jit(solution)/shard_map/dot_general | solution.py:183
  201.3 8.9 %all_to_all.42 = f32[8,1,512]{2,1,0:T(1,128)S(1)} all-to-all(f32[8,1,512]{2,1,0:T(1,128)S(1)} %reshape.258), channel_id=1, replica_groups=mesh['rows'=8,'scen'=4] {'rows'}, dimensions={0} | all-to-all | bytes 32768 | tf_op jit(solution)/shard_map/all_to_all | solution.py:186
  210.2 0.7 reduce.34
  211.2 0.9 fusion.65
  212.0 8.1 %reduce-scatter.2.cloned.1.call-done = f32[16,2048]{1,0:T(8,128)} async-done(((f32[64,2048]{1,0:T(8,128)}), f32[16,2048]{1,0:T(8,128)}) %reduce-scatter.2.cloned.1.call-update) | async-done | bytes 131088 | tf_op jit(solution)/shard_map/reduce_scatter | solution.py:184
  (178 shorter events, 25.1 us)
Async XLA Ops:
  7.2 48.7 %copy-start = (f32[16,2048]{1,0:T(8,128)S(1)}, f32[16,2048]{1,0:T(8,128)}, u32[]{:S(2)}) copy-start(f32[16,2048]{1,0:T(8,128)} %param.16) | copy-start | bytes 393220
  8.8 33.1 %copy-start.4 = (s32[128]{0:T(128)}, s32[128]{0:T(128)S(1)}, u32[]{:S(2)}) copy-start(s32[128]{0:T(128)S(1)} %fusion.143) | copy-start | bytes 1540
  11.1 32.9 %all-to-all-start.1 = ((f32[8,1,80]{2,1,0:T(1,128)}), f32[8,1,80]{2,1,0:T(1,128)S(1)}, u32[]{:S(2)}, u32[]{:S(2)}) async-start(f32[8,1,80]{2,1,0:T(1,128)} %bitcast.19), calls=%async_computation.1 | async-start | bytes 8192 | tf_op jit(solution)/shard_map/all_to_all | solution.py:73
  20.8 39.7 %collective-permute-start.1 = (f32[130,16]{0,1:T(8,128)S(1)}, f32[130,16]{0,1:T(8,128)S(1)}, u32[]{:S(2)}, u32[]{:S(2)}) collective-permute-start(f32[130,16]{0,1:T(8,128)S(1)} %pad_maximum_fusion.14), channel_id=1, source_target_pairs={{0,4},{4,0},{8,12},{12,8},{16,20},{20,16},{24,28},{28,24},{1,5},{5... | collective-permute-start | bytes 24968 | tf_op jit(solution)/shard_map/ppermute | solution.py:10
  38.7 4.1 %copy-start.6 = (u32[32]{0:T(128)S(1)}, u32[32]{0:T(128)}, u32[]{:S(2)}) copy-start(u32[32]{0:T(128)} %constant.102) | copy-start | bytes 388
  44.8 84.1 %all-to-all-start = ((f32[8,114,64]{1,2,0:T(8,128)}), f32[8,114,64]{1,2,0:T(8,128)S(1)}, u32[]{:S(2)}, u32[]{:S(2)}) async-start(f32[8,114,64]{1,2,0:T(8,128)} %bitcast.8), calls=%async_computation | async-start | bytes 524288 | tf_op jit(solution)/shard_map/all_to_all | solution.py:95
  49.3 41.4 %all-reduce.5.cloned.1.call-start = ((), (), s32[]{:S(2)}) async-start(), calls=%async_computation.8 | async-start | bytes 696320 | tf_op jit(solution)/shard_map/psum | solution.py:119
  56.9 68.2 %all-reduce.7.cloned.1.call-start = ((), (), s32[]{:S(2)}) async-start(), calls=%async_computation.9 | async-start | bytes 196608 | tf_op jit(solution)/shard_map/psum | solution.py:123
  57.7 74.1 %collective-permute-start = (f32[16,272]{1,0:T(8,128)S(1)}, f32[16,272]{1,0:T(8,128)S(1)}, u32[]{:S(2)}, u32[]{:S(2)}) collective-permute-start(f32[16,272]{1,0:T(8,128)S(1)} %fusion.39), channel_id=1, source_target_pairs={{0,4},{4,0},{8,12},{12,8},{16,20},{20,16},{24,28},{28,24},{1,5},{5... | collective-permute-start | bytes 52232 | tf_op jit(solution)/shard_map/ppermute | solution.py:10
  90.7 37.8 %copy-start.1 = (bf16[544,272]{0,1:T(8,128)(2,1)S(1)}, bf16[544,272]{0,1:T(8,128)(2,1)}, u32[]{:S(2)}) copy-start(bf16[544,272]{0,1:T(8,128)(2,1)} %all-reduce.5.cloned.1.call-done) | copy-start | bytes 887812
  92.0 36.2 %collective-permute-start.2 = (bf16[272,272]{0,1:T(8,128)(2,1)S(1)}, bf16[272,272]{0,1:T(8,128)(2,1)S(1)}, u32[]{:S(2)}, u32[]{:S(2)}) collective-permute-start(bf16[272,272]{0,1:T(8,128)(2,1)S(1)} %get-tuple-element.22), channel_id=1, source_target_pairs={{0,4},{4,0},{8,12},{12,8},{16,20},{20,16},{24,28},{28,24},{1,5},{5... | collective-permute-start | bytes 443912 | tf_op jit(solution)/shard_map/ppermute | solution.py:10
  125.9 6.0 %collective-permute-start.3 = (f32[16,273]{1,0:T(8,128)S(1)}, f32[16,273]{1,0:T(8,128)}, u32[]{:S(2)}, u32[]{:S(2)}) collective-permute-start(f32[16,273]{1,0:T(8,128)S(1)} %constant_dynamic-slice_fusion), channel_id=1, source_target_pairs={{0,4},{4,0},{8,12},{12,8},{16,20},{20,16},{24,28},{28,24},{1,5},{5... | collective-permute-start | bytes 52424 | tf_op jit(solution)/shard_map/ppermute | solution.py:10
  131.3 3.9 %copy-start.2 = (f32[16,16]{1,0:T(8,128)S(1)}, f32[16,16]{1,0:T(8,128)}, u32[]{:S(2)}) copy-start(f32[16,16]{1,0:T(8,128)} %get-tuple-element.59) | copy-start | bytes 3076
  131.3 3.9 %copy-start.3 = (pred[544]{0:T(1024)(128)(4,1)S(1)}, pred[544]{0:T(1024)(128)(4,1)}, u32[]{:S(2)}) copy-start(pred[544]{0:T(1024)(128)(4,1)} %broadcast_compare_fusion) | copy-start | bytes 1636
  137.3 11.0 %all-to-all-start.3 = ((f32[8,1,128]{2,1,0:T(1,128)}), f32[8,1,128]{2,1,0:T(1,128)S(1)}, u32[]{:S(2)}, u32[]{:S(2)}) async-start(f32[8,1,128]{2,1,0:T(1,128)} %reshape.252), calls=%async_computation.3 | async-start | bytes 8192 | tf_op jit(solution)/shard_map/all_to_all | solution.py:177
  148.3 9.6 %all-to-all-start.2 = ((f32[8,1,128]{2,1,0:T(1,128)}), f32[8,1,128]{2,1,0:T(1,128)S(1)}, u32[]{:S(2)}, u32[]{:S(2)}) async-start(f32[8,1,128]{2,1,0:T(1,128)} %reshape.250), calls=%async_computation.2 | async-start | bytes 8192 | tf_op jit(solution)/shard_map/all_to_all | solution.py:177
  162.5 9.6 %all-to-all-start.5 = ((f32[8,1,128]{2,1,0:T(1,128)}), f32[8,1,128]{2,1,0:T(1,128)S(1)}, u32[]{:S(2)}, u32[]{:S(2)}) async-start(f32[8,1,128]{2,1,0:T(1,128)} %reshape.256), calls=%async_computation.5 | async-start | bytes 8192 | tf_op jit(solution)/shard_map/all_to_all | solution.py:177
  172.2 9.6 %all-to-all-start.4 = ((f32[8,1,128]{2,1,0:T(1,128)}), f32[8,1,128]{2,1,0:T(1,128)S(1)}, u32[]{:S(2)}, u32[]{:S(2)}) async-start(f32[8,1,128]{2,1,0:T(1,128)} %reshape.254), calls=%async_computation.4 | async-start | bytes 8192 | tf_op jit(solution)/shard_map/all_to_all | solution.py:177
  175.5 44.6 %reduce-scatter.2.cloned.1.call-start = ((), (), s32[]{:S(2)}) async-start(), calls=%async_computation.10 | async-start | bytes 655360 | tf_op jit(solution)/shard_map/reduce_scatter | solution.py:184
  196.7 14.5 %copy-start.5 = (s32[128]{0:T(128)S(1)}, s32[128]{0:T(128)}, u32[]{:S(2)}) copy-start(s32[128]{0:T(128)} %copy-done.4) | copy-start | bytes 1540
Sparse Core Ops, SparseCore 0:
  57.1 33.6 all-reduce.4
  93.6 31.4 all-reduce.6
  201.1 18.9 reduce-scatter.1
where the time goes:
time: 228 us; the launch traced here: 227 us
  waiting for transfers between devices  88.3 us (39%)
  starting transfers between devices  33.7 us (15%)
  blocking collectives  30.7 us (13%)
  matrix products  24.3 us (11%)
  local copies, waits for them, and re-layouts  21.1 us (9%)
  between operations  15 us (7%)
  other arithmetic  13.6 us (6%)
    psum x1, waiting for transfers between devices, per_device(): side = lax.psum(jnp.concatenate([pts_part, depth_part], 1), 'scen')  31.6 us
    psum x1, waiting for transfers between devices, per_device(): own_cols = lax.psum(part, 'scen')  27.9 us
    all_to_all x4, waiting for transfers between devices, per_device(): lax.all_to_all(out.reshape(n, 2, scen, 2 * ends // n), 'rows', 0, 0, tile...  20.7 us
    all_to_all x4, starting transfers between devices, per_device(): lax.all_to_all(out.reshape(n, 2, scen, 2 * ends // n), 'rows', 0, 0, tile...  14.5 us
    all_to_all x1, blocking collectives, per_device(): lax.all_to_all(own_current.reshape(scen, n, slots).transpose(1, 0, 2), 'r...  8.94 us
    dot_general x9, matrix products, exact_dot(): return jnp.dot(left, right, precision=lax.Precision.HIGHEST)  8.49 us
    reduce_scatter x1, waiting for transfers between devices, per_device(): voltage = lax.psum_scatter(partial, 'scen', scatter_dimension=0, tiled=True)  8.07 us
    all_to_all x1, starting transfers between devices, per_device(): lax.all_to_all(jnp.concatenate([bus_out, ends_out], 1), 'rows', 0, 0, til...  7.28 us
  transfers between devices with their start and end apart: 13, of which 7 were waited for; matrix products, arithmetic and copies ran while one was open for 17% of the time, Pallas kernels for 0%

commit v1 on v0

--- a/solution.py
+++ b/solution.py
@@ -2,6 +2,10 @@
 import jax.numpy as jnp
 from jax import lax
 from jax.sharding import PartitionSpec as P
+
+
+def apply_surface_here(tile_in, axis_id):
+    return jnp.sum(jax.lax.all_gather(tile_in, axis_id), 0)
 
 
 def swapped(value, axis, apart):
@@ -120,7 +124,7 @@
     branch_part = jnp.dot(picks, inverse, preferred_element_type=f32)
     pts_part = jnp.dot(picks, narrow, preferred_element_type=f32)
     depth_part = jnp.sum(branch_part * col_picks, axis=1, keepdims=True)
-    side = lax.psum(jnp.concatenate([pts_part, depth_part], 1), "scen")
+    side = apply_surface_here(jnp.concatenate([pts_part, depth_part], 1), "scen")
     side = lax.dynamic_slice_in_dim(side, share * scen, scen, axis=0)
     own_diag = lax.dynamic_slice_in_dim(own_cols, half * hp, hp, axis=0)
     cross = lax.dynamic_slice_in_dim(own_cols, (1 - half) * hp, hp, axis=0).T

time: 228 us -> 211 us (0.925)
  waiting for transfers between devices: 88.3 us -> 63.4 us
  blocking collectives: 30.7 us -> 37.9 us
    psum x1 -> x0, waiting for transfers between devices: 31.6 us -> none  [per_device(): side = lax.psum(jnp.concatenate([pts_part, depth_part], 1), 'scen')]
    all_gather x0 -> x1, blocking collectives: none -> 6.63 us  [apply_surface_here(): return jnp.sum(jax.lax.all_gather(tile_in, axis_id), 0)]
    psum x1, waiting for transfers between devices: 27.9 us -> 31.7 us  [per_device(): own_cols = lax.psum(part, 'scen')]
    ppermute x4, waiting for transfers between devices: 0.01 us -> 3.51 us  [swapped(): return lax.ppermute(value, axis, pairs)]
  transfers between devices with their start and end apart: 13 -> 12, of which waited for: 7 -> 7; matrix products, arithmetic and copies ran while one was open for 17% -> 18% of each run, Pallas kernels for 0% -> 0%
where the time goes in v1:
time: 211 us; the launch traced here: 209 us
  waiting for transfers between devices  63.4 us (30%)
  blocking collectives  37.9 us (18%)
  starting transfers between devices  33.2 us (16%)
  matrix products  24.9 us (12%)
  local copies, waits for them, and re-layouts  20.9 us (10%)
  between operations  15.3 us (7%)
  other arithmetic  13.8 us (7%)
    psum x1, waiting for transfers between devices, per_device(): own_cols = lax.psum(part, 'scen')  31.7 us
    all_to_all x4, waiting for transfers between devices, per_device(): lax.all_to_all(out.reshape(n, 2, scen, 2 * ends // n), 'rows', 0, 0, tile...  20.7 us
    all_to_all x4, starting transfers between devices, per_device(): lax.all_to_all(out.reshape(n, 2, scen, 2 * ends // n), 'rows', 0, 0, tile...  15.7 us
    dot_general x9, matrix products, exact_dot(): return jnp.dot(left, right, precision=lax.Precision.HIGHEST)  9.12 us
    all_to_all x1, blocking collectives, per_device(): lax.all_to_all(own_current.reshape(scen, n, slots).transpose(1, 0, 2), 'r...  8.94 us
    reduce_scatter x1, waiting for transfers between devices, per_device(): voltage = lax.psum_scatter(partial, 'scen', scatter_dimension=0, tiled=True)  7.48 us
    all_to_all x1, starting transfers between devices, per_device(): lax.all_to_all(jnp.concatenate([bus_out, ends_out], 1), 'rows', 0, 0, til...  7.28 us
    unnamed x1, blocking collectives  6.67 us
  transfers between devices with their start and end apart: 12, of which 7 were waited for; matrix products, arithmetic and copies ran while one was open for 18% of the time, Pallas kernels for 0%

profile of v1, /device:TPU:0, one launch (start us, length us, event | category | flops | bytes accessed | tf_op | source)
XLA Modules:
  0.0 209.4 jit_solution(11268933911044145062)
XLA Ops:
  7.2 0.9 convert_reduce_fusion.1
  9.5 1.0 fusion.71
  11.1 7.3 %all-to-all-start.1 = ((f32[8,1,80]{2,1,0:T(1,128)}), f32[8,1,80]{2,1,0:T(1,128)S(1)}, u32[]{:S(2)}, u32[]{:S(2)}) async-start(f32[8,1,80]{2,1,0:T(1,128)} %bitcast.19), calls=%async_computation.1 | async-start | bytes 8192 | tf_op jit(solution)/shard_map/all_to_all | solution.py:77
  18.4 0.7 copy.254
  19.9 0.9 copy.309
  20.8 2.0 collective-permute-start.1
  23.7 5.2 %all-gather.1 = s32[1,64,4]{2,0,1:T(1,128)S(1)} all-gather(s32[1,16,4]{2,0,1:T(1,128)S(1)} %copy.320), channel_id=3, replica_groups=mesh['rows'=8,'scen'=4] {'scen'}, dimensions={1}, use_global_device_ids=true | all-gather | bytes 1280 | tf_op jit(solution)/shard_map/all_gather | solution.py:110
  29.0 5.2 %all-gather = s32[1,64,4]{2,0,1:T(1,128)S(1)} all-gather(s32[1,16,4]{2,0,1:T(1,128)S(1)} %copy.319), channel_id=2, replica_groups=mesh['rows'=8,'scen'=4] {'scen'}, dimensions={1}, use_global_device_ids=true | all-gather | bytes 1280 | tf_op jit(solution)/shard_map/all_gather | solution.py:107
  34.2 1.3 dynamic-slice_reduce_fusion
  35.5 1.3 dynamic-slice_reduce_fusion.1
  37.5 1.2 fusion.66
  38.7 3.2 %multiply_reduce_fusion = (f32[64]{0:T(128)S(1)}, f32[64,2048]{1,0:T(8,128)S(1)}) fusion(s32[2048]{0:T(1024)S(1)} %iota_add_fusion, s32[64]{0:T(128)S(1)} %dynamic-slice_reduce_fusion, s32[64]{0:T(128)S(1)} %dynamic-slice_reduce_fusion.1, bf16[1024,2048]{1,0:T(8,128)(2,1)} %param.15, s32[1024]{0:T(1024)S(1)} %iota_add_fusion.1), kind=kOutput, calls=%fused_computation.54 | convolution fusion | flops 269680576 | bytes 4731648 | tf_op jit(solution)/shard_map/dot_general | solution.py:124
  44.0 0.7 broadcast_in_dim.170
  44.8 4.5 %all-to-all-start = ((f32[8,114,64]{1,2,0:T(8,128)}), f32[8,114,64]{1,2,0:T(8,128)S(1)}, u32[]{:S(2)}, u32[]{:S(2)}) async-start(f32[8,114,64]{1,2,0:T(8,128)} %bitcast.8), calls=%async_computation | async-start | bytes 524288 | tf_op jit(solution)/shard_map/all_to_all | solution.py:99
  49.7 4.1 %fusion.16 = bf16[272,1024]{1,0:T(8,128)(2,1)S(1)} fusion(bf16[1024,2048]{1,0:T(8,128)(2,1)} %param.15, s32[272]{0:T(512)S(1)} %fusion.142), kind=kOutput, calls=%fused_computation.21 | convolution fusion | flops 1142243328 | bytes 4752448 | tf_op jit(solution)/shard_map/dot_general | solution.py:121
  54.2 6.6 %all-gather.2 = f32[256,273]{1,0:T(8,128)S(1)} all-gather(f32[64,273]{1,0:T(8,128)S(1)} %pad_maximum_fusion.12), channel_id=4, replica_groups=mesh['rows'=8,'scen'=4] {'scen'}, dimensions={0}, use_global_device_ids=true | all-gather | bytes 349440 | tf_op jit(solution)/shard_map/all_gather | solution.py:8
  62.4 1.5 fusion.19
  63.8 2.0 collective-permute-start.3
  66.4 1.6 fusion.39
  69.8 31.7 %all-reduce.4.cloned.1.call-done = bf16[544,272]{0,1:T(8,128)(2,1)} async-done(((bf16[544,272]{0,1:T(8,128)(2,1)}), bf16[544,272]{0,1:T(8,128)(2,1)}) %all-reduce.4.cloned.1.call-update) | async-done | bytes 295952 | tf_op jit(solution)/shard_map/psum | solution.py:123
  101.5 1.3 constant_dynamic-slice_fusion.4
  102.9 1.5 collective-permute-start.2
  105.2 3.5 %collective-permute-done.2 = bf16[272,272]{0,1:T(8,128)(2,1)S(1)} collective-permute-done((bf16[272,272]{0,1:T(8,128)(2,1)S(1)}, bf16[272,272]{0,1:T(8,128)(2,1)S(1)}, u32[]{:S(2)}, u32[]{:S(2)}) %collective-permute-start.2) | collective-permute-done | bytes 148000 | tf_op jit(solution)/shard_map/ppermute | solution.py:14
  109.3 1.2 pad_slice_fusion.1
  110.5 1.1 copy.307
  112.3 0.9 fusion.105
  113.2 1.6 multiply_reduce_fusion.6
  115.1 0.9 fusion.135
  116.4 0.8 multiply_reduce_fusion.5
  118.6 5.8 %all-to-all-start.3 = ((f32[8,1,128]{2,1,0:T(1,128)}), f32[8,1,128]{2,1,0:T(1,128)S(1)}, u32[]{:S(2)}, u32[]{:S(2)}) async-start(f32[8,1,128]{2,1,0:T(1,128)} %reshape.253), calls=%async_computation.3 | async-start | bytes 8192 | tf_op jit(solution)/shard_map/all_to_all | solution.py:181
  125.5 5.2 %all-to-all-done.3 = f32[8,1,128]{2,1,0:T(1,128)S(1)} async-done(((f32[8,1,128]{2,1,0:T(1,128)}), f32[8,1,128]{2,1,0:T(1,128)S(1)}, u32[]{:S(2)}, u32[]{:S(2)}) %all-to-all-start.3) | async-done | bytes 4128 | tf_op jit(solution)/shard_map/all_to_all | solution.py:181
  130.8 3.3 %all-to-all-start.2 = ((f32[8,1,128]{2,1,0:T(1,128)}), f32[8,1,128]{2,1,0:T(1,128)S(1)}, u32[]{:S(2)}, u32[]{:S(2)}) async-start(f32[8,1,128]{2,1,0:T(1,128)} %reshape.251), calls=%async_computation.2 | async-start | bytes 8192 | tf_op jit(solution)/shard_map/all_to_all | solution.py:181
  135.7 4.7 %all-to-all-done.2 = f32[8,1,128]{2,1,0:T(1,128)S(1)} async-done(((f32[8,1,128]{2,1,0:T(1,128)}), f32[8,1,128]{2,1,0:T(1,128)S(1)}, u32[]{:S(2)}, u32[]{:S(2)}) %all-to-all-start.2) | async-done | bytes 4128 | tf_op jit(solution)/shard_map/all_to_all | solution.py:181
  141.5 0.8 multiply_reduce_fusion.4
  142.8 0.8 multiply_reduce_fusion.3
  145.0 3.3 %all-to-all-start.5 = ((f32[8,1,128]{2,1,0:T(1,128)}), f32[8,1,128]{2,1,0:T(1,128)S(1)}, u32[]{:S(2)}, u32[]{:S(2)}) async-start(f32[8,1,128]{2,1,0:T(1,128)} %reshape.257), calls=%async_computation.5 | async-start | bytes 8192 | tf_op jit(solution)/shard_map/all_to_all | solution.py:181
  149.1 5.5 %all-to-all-done.5 = f32[8,1,128]{2,1,0:T(1,128)S(1)} async-done(((f32[8,1,128]{2,1,0:T(1,128)}), f32[8,1,128]{2,1,0:T(1,128)S(1)}, u32[]{:S(2)}, u32[]{:S(2)}) %all-to-all-start.5) | async-done | bytes 4128 | tf_op jit(solution)/shard_map/all_to_all | solution.py:181
  154.6 3.3 %all-to-all-start.4 = ((f32[8,1,128]{2,1,0:T(1,128)}), f32[8,1,128]{2,1,0:T(1,128)S(1)}, u32[]{:S(2)}, u32[]{:S(2)}) async-start(f32[8,1,128]{2,1,0:T(1,128)} %reshape.255), calls=%async_computation.4 | async-start | bytes 8192 | tf_op jit(solution)/shard_map/all_to_all | solution.py:181
  159.0 5.3 %all-to-all-done.4 = f32[8,1,128]{2,1,0:T(1,128)S(1)} async-done(((f32[8,1,128]{2,1,0:T(1,128)}), f32[8,1,128]{2,1,0:T(1,128)S(1)}, u32[]{:S(2)}, u32[]{:S(2)}) %all-to-all-start.4) | async-done | bytes 4128 | tf_op jit(solution)/shard_map/all_to_all | solution.py:181
  165.3 0.8 multiply_reduce_fusion.2
  166.6 0.8 multiply_reduce_fusion.1
  167.3 5.3 %all_gather.22 = bf16[64,544]{1,0:T(8,128)(2,1)S(1)} all-gather(bf16[16,544]{1,0:T(8,128)(2,1)S(1)} %get-tuple-element.76), channel_id=1, replica_groups=mesh['rows'=8,'scen'=4] {'scen'}, dimensions={0}, use_global_device_ids=true | all-gather | bytes 87040 | tf_op jit(solution)/shard_map/all_gather | solution.py:184
  173.1 6.7 %all-reduce.1 = f32[64]{0:T(128)S(1)} all-reduce(f32[64]{0:T(128)S(1)} %dynamic-update-slice), channel_id=1, replica_groups=mesh['rows'=8,'scen'=4] {'scen'}, use_global_device_ids=true, to_apply=%add.1 | all-reduce | flops 64 | bytes 512
  179.7 4.3 %convolution_subtract_fusion = f32[64,2048]{1,0:T(8,128)} fusion(bf16[1024,2048]{1,0:T(8,128)(2,1)} %param.15, bf16[64,544]{1,0:T(8,128)(2,1)S(1)} %all_gather.22, s32[1024]{0:T(1024)S(1)} %iota_add_fusion.1, s32[544]{0:T(1024)S(1)} %select_n.202, f32[64,2048]{1,0:T(8,128)S(1)} %get-tuple-element.65, f32[64]{0:T(128)S(1)} %all-reduce.1), kind=kOutput, calls=%fused_computation.7 | convolution fusion | flops 340623360 | bytes 5319040 | tf_op jit(solution)/shard_map/dot_general | solution.py:187
  184.3 8.9 %all_to_all.42 = f32[8,1,512]{2,1,0:T(1,128)S(1)} all-to-all(f32[8,1,512]{2,1,0:T(1,128)S(1)} %reshape.259), channel_id=1, replica_groups=mesh['rows'=8,'scen'=4] {'rows'}, dimensions={0} | all-to-all | bytes 32768 | tf_op jit(solution)/shard_map/all_to_all | solution.py:190
  193.3 0.7 reduce.34
  194.2 0.9 fusion.65
  195.1 7.5 %reduce-scatter.2.cloned.1.call-done = f32[16,2048]{1,0:T(8,128)} async-done(((f32[64,2048]{1,0:T(8,128)}), f32[16,2048]{1,0:T(8,128)}) %reduce-scatter.2.cloned.1.call-update) | async-done | bytes 131088 | tf_op jit(solution)/shard_map/reduce_scatter | solution.py:188
  (177 shorter events, 24.7 us)
Async XLA Ops:
  7.2 59.2 %copy-start = (f32[16,2048]{1,0:T(8,128)S(1)}, f32[16,2048]{1,0:T(8,128)}, u32[]{:S(2)}) copy-start(f32[16,2048]{1,0:T(8,128)} %param.16) | copy-start | bytes 393220
  8.8 33.1 %copy-start.4 = (s32[128]{0:T(128)}, s32[128]{0:T(128)S(1)}, u32[]{:S(2)}) copy-start(s32[128]{0:T(128)S(1)} %fusion.143) | copy-start | bytes 1540
  11.1 32.9 %all-to-all-start.1 = ((f32[8,1,80]{2,1,0:T(1,128)}), f32[8,1,80]{2,1,0:T(1,128)S(1)}, u32[]{:S(2)}, u32[]{:S(2)}) async-start(f32[8,1,80]{2,1,0:T(1,128)} %bitcast.19), calls=%async_computation.1 | async-start | bytes 8192 | tf_op jit(solution)/shard_map/all_to_all | solution.py:77
  20.8 47.3 %collective-permute-start.1 = (f32[130,16]{0,1:T(8,128)S(1)}, f32[130,16]{0,1:T(8,128)S(1)}, u32[]{:S(2)}, u32[]{:S(2)}) collective-permute-start(f32[130,16]{0,1:T(8,128)S(1)} %pad_maximum_fusion.14), channel_id=1, source_target_pairs={{0,4},{4,0},{8,12},{12,8},{16,20},{20,16},{24,28},{28,24},{1,5},{5... | collective-permute-start | bytes 24968 | tf_op jit(solution)/shard_map/ppermute | solution.py:14
  38.7 4.1 %copy-start.6 = (u32[32]{0:T(128)S(1)}, u32[32]{0:T(128)}, u32[]{:S(2)}) copy-start(u32[32]{0:T(128)} %constant.102) | copy-start | bytes 388
  44.8 64.5 %all-to-all-start = ((f32[8,114,64]{1,2,0:T(8,128)}), f32[8,114,64]{1,2,0:T(8,128)S(1)}, u32[]{:S(2)}, u32[]{:S(2)}) async-start(f32[8,114,64]{1,2,0:T(8,128)} %bitcast.8), calls=%async_computation | async-start | bytes 524288 | tf_op jit(solution)/shard_map/all_to_all | solution.py:99
  49.3 52.2 %all-reduce.4.cloned.1.call-start = ((), (), s32[]{:S(2)}) async-start(), calls=%async_computation.8 | async-start | bytes 696320 | tf_op jit(solution)/shard_map/psum | solution.py:123
  63.8 49.3 %collective-permute-start.3 = (f32[16,273]{1,0:T(8,128)}, f32[16,273]{1,0:T(8,128)}, u32[]{:S(2)}, u32[]{:S(2)}) collective-permute-start(f32[16,273]{1,0:T(8,128)} %constant_dynamic-slice_fusion), channel_id=1, source_target_pairs={{0,4},{4,0},{8,12},{12,8},{16,20},{20,16},{24,28},{28,24},{1,5},{5... | collective-permute-start | bytes 52424 | tf_op jit(solution)/shard_map/ppermute | solution.py:14
  68.0 44.2 %collective-permute-start = (f32[16,272]{1,0:T(8,128)}, f32[16,272]{1,0:T(8,128)}, u32[]{:S(2)}, u32[]{:S(2)}) collective-permute-start(f32[16,272]{1,0:T(8,128)} %fusion.39), channel_id=1, source_target_pairs={{0,4},{4,0},{8,12},{12,8},{16,20},{20,16},{24,28},{28,24},{1,5},{5... | collective-permute-start | bytes 52232 | tf_op jit(solution)/shard_map/ppermute | solution.py:14
  101.5 7.4 %copy-start.1 = (bf16[544,272]{0,1:T(8,128)(2,1)S(1)}, bf16[544,272]{0,1:T(8,128)(2,1)}, u32[]{:S(2)}) copy-start(bf16[544,272]{0,1:T(8,128)(2,1)} %all-reduce.4.cloned.1.call-done) | copy-start | bytes 887812
  102.9 5.9 %collective-permute-start.2 = (bf16[272,272]{0,1:T(8,128)(2,1)S(1)}, bf16[272,272]{0,1:T(8,128)(2,1)S(1)}, u32[]{:S(2)}, u32[]{:S(2)}) collective-permute-start(bf16[272,272]{0,1:T(8,128)(2,1)S(1)} %get-tuple-element.22), channel_id=1, source_target_pairs={{0,4},{4,0},{8,12},{12,8},{16,20},{20,16},{24,28},{28,24},{1,5},{5... | collective-permute-start | bytes 443912 | tf_op jit(solution)/shard_map/ppermute | solution.py:14
  111.7 4.7 %copy-start.2 = (f32[16,16]{1,0:T(8,128)S(1)}, f32[16,16]{1,0:T(8,128)}, u32[]{:S(2)}) copy-start(f32[16,16]{1,0:T(8,128)} %get-tuple-element.59) | copy-start | bytes 3076
  111.7 4.7 %copy-start.3 = (pred[544]{0:T(1024)(128)(4,1)S(1)}, pred[544]{0:T(1024)(128)(4,1)}, u32[]{:S(2)}) copy-start(pred[544]{0:T(1024)(128)(4,1)} %broadcast_compare_fusion) | copy-start | bytes 1636
  118.6 12.2 %all-to-all-start.3 = ((f32[8,1,128]{2,1,0:T(1,128)}), f32[8,1,128]{2,1,0:T(1,128)S(1)}, u32[]{:S(2)}, u32[]{:S(2)}) async-start(f32[8,1,128]{2,1,0:T(1,128)} %reshape.253), calls=%async_computation.3 | async-start | bytes 8192 | tf_op jit(solution)/shard_map/all_to_all | solution.py:181
  130.8 9.6 %all-to-all-start.2 = ((f32[8,1,128]{2,1,0:T(1,128)}), f32[8,1,128]{2,1,0:T(1,128)S(1)}, u32[]{:S(2)}, u32[]{:S(2)}) async-start(f32[8,1,128]{2,1,0:T(1,128)} %reshape.251), calls=%async_computation.2 | async-start | bytes 8192 | tf_op jit(solution)/shard_map/all_to_all | solution.py:181
  145.0 9.6 %all-to-all-start.5 = ((f32[8,1,128]{2,1,0:T(1,128)}), f32[8,1,128]{2,1,0:T(1,128)S(1)}, u32[]{:S(2)}, u32[]{:S(2)}) async-start(f32[8,1,128]{2,1,0:T(1,128)} %reshape.257), calls=%async_computation.5 | async-start | bytes 8192 | tf_op jit(solution)/shard_map/all_to_all | solution.py:181
  154.6 9.6 %all-to-all-start.4 = ((f32[8,1,128]{2,1,0:T(1,128)}), f32[8,1,128]{2,1,0:T(1,128)S(1)}, u32[]{:S(2)}, u32[]{:S(2)}) async-start(f32[8,1,128]{2,1,0:T(1,128)} %reshape.255), calls=%async_computation.4 | async-start | bytes 8192 | tf_op jit(solution)/shard_map/all_to_all | solution.py:181
  157.9 44.6 %reduce-scatter.2.cloned.1.call-start = ((), (), s32[]{:S(2)}) async-start(), calls=%async_computation.9 | async-start | bytes 655360 | tf_op jit(solution)/shard_map/reduce_scatter | solution.py:188
  179.7 14.5 %copy-start.5 = (s32[128]{0:T(128)S(1)}, s32[128]{0:T(128)}, u32[]{:S(2)}) copy-start(s32[128]{0:T(128)} %copy-done.4) | copy-start | bytes 1540
Sparse Core Ops, SparseCore 0:
  68.2 33.2 all-reduce.3
  184.2 18.3 reduce-scatter.1
